TPU v7x, 512 devices: a whole 4x8x8 slice. The times are simulated.
512 devices in a mesh: dp: 64 (over z, x, core), group: 8 (over y).
Axes of the slice: x: 4, y: 8, z: 8, core: 2. Of those that a mesh axis runs over, the one named last changes fastest.
Arguments:
- embeddings: bfloat16 [32768, 1024], P(('dp', 'group')), may hold values from -6 to 6
- cluster_ids: int32 [32768, 1], P(('dp', 'group')), may hold values from 0 to 63; in each aligned block of 64 rows (0 to 63, 64 to 127, ...) at most 2 rows name the same one
Outputs:
- density: float32 [32768], P(('dp', 'group'))
Inputs may be any that keep to these rules, and one draw needn't show every extreme that they name: `cluster_ids`: among the 64 documents of one device no cluster appears more than 2 times, and some cluster appears exactly 2 times; every cluster appears somewhere.
All inputs are finite; a program needn't handle non-finite values.
Results may differ from a plain program's by a relative error of at most 0.0031.
Values may be sent and summed in bfloat16 or wider, within the bound.
A program may use at most 64 MiB of HBM per device.

v0:
```python
import math

import jax
import jax.numpy as jnp
from jax import lax
from jax.sharding import PartitionSpec as P

epsilon = 1e-06


def pair_scores(left_rows, right_rows, sharpen):
    scores = lax.dot_general(
        left_rows, right_rows, (((1,), (1,)), ((), ())), preferred_element_type=jnp.float32
    )
    return jnp.exp(scores * sharpen)


def shards(embeddings, cluster_ids):
    owners = lax.axis_size("dp")
    group_size = lax.axis_size("group")
    group_index = lax.axis_index("group")
    doc_rows, width = embeddings.shape
    per_owner = 2 * doc_rows // owners
    slot_count = owners * per_owner
    sharpen = math.sqrt(width)
    widened = embeddings.astype(jnp.float32)
    normed = (
        widened / jnp.sqrt(jnp.sum(widened * widened, axis=1, keepdims=True) + epsilon)
    ).astype(jnp.bfloat16)
    cluster = cluster_ids[:, 0]
    one_hot = (cluster[:, None] == jnp.arange(owners, dtype=jnp.int32)[None, :]).astype(jnp.int32)
    running = jnp.cumsum(one_hot, axis=0)
    within = jnp.sum(running * one_hot, axis=1) - 1
    slot_index = cluster * per_owner + within
    outgoing = (
        jnp.zeros((slot_count, width), jnp.bfloat16)
        .at[slot_index]
        .set(normed)
        .reshape(owners, per_owner, width)
    )
    occupied = (
        jnp.zeros((slot_count,), jnp.bfloat16)
        .at[slot_index]
        .set(jnp.ones((doc_rows,), jnp.bfloat16))
        .reshape(owners, per_owner)
    )
    received, flags = (
        lax.all_to_all(outgoing, "dp", split_axis=0, concat_axis=0, tiled=True),
        lax.all_to_all(occupied, "dp", split_axis=0, concat_axis=0, tiled=True),
    )
    member_rows = received.reshape(slot_count, width)
    live_flags = flags.reshape(slot_count)
    own_index = group_index * slot_count + jnp.arange(slot_count, dtype=jnp.int32)
    piece_rows = lax.all_gather(member_rows, "group", axis=0, tiled=True)
    piece_flags = lax.all_gather(live_flags, "group", axis=0, tiled=True)
    piece_count = piece_rows.shape[0]
    column_index = jnp.arange(piece_count, dtype=jnp.int32)
    distinct = own_index[:, None] != column_index[None, :]
    weights = jnp.where(distinct, pair_scores(member_rows, piece_rows, sharpen), 0.0)
    weights = weights * piece_flags.astype(jnp.float32)[None, :]
    row_sums = jnp.sum(weights, axis=1)
    scaled = (row_sums / (doc_rows * group_size)).reshape(owners, per_owner)
    returned = lax.all_to_all(scaled, "dp", split_axis=0, concat_axis=0, tiled=True)
    return returned.reshape(slot_count)[slot_index]


def solution(mesh):
    placed = (P(("dp", "group"), None), P(("dp", "group"), None))
    return jax.shard_map(
        shards, mesh=mesh, in_specs=placed, out_specs=P(("dp", "group")), check_vma=False
    )
```

profile of v0, /device:TPU:1, one launch (start us, length us, event | category | flops | bytes accessed | tf_op | source)
XLA Modules:
  0.0 112.3 jit_solution(4247048955436508361)
XLA Ops:
  6.5 0.0 all-gather.3.cloned.1.call-start
  6.5 1.0 fusion.4
  7.6 0.7 fusion.10
  8.3 0.1 reduce_window_sum.11
  8.4 0.8 select_reduce_fusion
  9.3 0.7 fusion.11
  9.9 1.4 %scatter_custom_fusion = bf16[128,1024]{1,0:T(8,128)(2,1)S(1)} fusion(s32[64]{0:T(128)S(1)} %fusion.11, bf16[64,1024]{1,0:T(8,128)(2,1)} %param.2, f32[64]{0:T(128)S(1)} %add_sqrt_fusion, bf16[]{:T(256)} %constant.13.clone.1), kind=kCustom, calls=%fused_computation.13 | custom fusion | flops 196608 | bytes 393730 | tf_op jit(solution)/shard_map/scatter | solution.py:38
  11.3 0.1 reshape.54
  11.4 27.7 %all_to_all.21 = bf16[64,2,1024]{2,1,0:T(2,128)(2,1)S(1)} all-to-all(bf16[64,2,1024]{2,1,0:T(2,128)(2,1)S(1)} %reshape.54), channel_id=1, replica_groups=mesh['dp'=64,'group'=8] {'dp'}, dimensions={0} | all-to-all | bytes 524288 | tf_op jit(solution)/shard_map/all_to_all | solution.py:48
  39.1 0.8 reshape.55
  40.0 0.0 all-gather.3.cloned.1.call-update
  40.0 1.0 scatter_custom_fusion.1
  41.0 0.8 all_to_all.17
  41.7 4.8 %all-to-all-start.1 = ((bf16[64,1,2]{2,1,0:T(2,128)(2,1)}), bf16[64,1,2]{2,1,0:T(2,128)(2,1)S(1)}, u32[]{:S(2)}, u32[]{:S(2)}) async-start(bf16[64,1,2]{2,1,0:T(2,128)(2,1)} %all_to_all.17), calls=%async_computation.1 | async-start | bytes 65536 | tf_op jit(solution)/shard_map/all_to_all | solution.py:49
  46.5 9.4 %all-to-all-done.1 = bf16[64,1,2]{2,1,0:T(2,128)(2,1)S(1)} async-done(((bf16[64,1,2]{2,1,0:T(2,128)(2,1)}), bf16[64,1,2]{2,1,0:T(2,128)(2,1)S(1)}, u32[]{:S(2)}, u32[]{:S(2)}) %all-to-all-start.1) | async-done | bytes 288 | tf_op jit(solution)/shard_map/all_to_all | solution.py:49
  55.9 0.1 reduce
  56.0 0.1 reshape.82
  56.2 14.2 %all-gather = bf16[8,1,128]{2,1,0:T(2,128)(2,1)S(1)} all-gather(bf16[1,1,128]{2,1,0:T(2,128)(2,1)S(1)} %reshape.82), channel_id=1, replica_groups=mesh['dp'=64,'group'=8] {'group'}, dimensions={0}, use_global_device_ids=true | all-gather | bytes 2304 | tf_op jit(solution)/shard_map/all_gather | solution.py:55
  70.4 4.3 %all-gather.3.cloned.1.call-done = bf16[1024,1024]{1,0:T(8,128)(2,1)} async-done(((bf16[128,1024]{1,0:T(8,128)(2,1)}), bf16[1024,1024]{1,0:T(8,128)(2,1)}) %all-gather.3.cloned.1.call-update) | async-done | bytes 2097168 | tf_op jit(solution)/shard_map/all_gather | solution.py:54
  74.7 2.7 %fusion.3 = f32[128]{0:T(128)S(1)} fusion(bf16[128,1024]{1,0:T(8,128)(2,1)} %reshape.55, bf16[1024,1024]{1,0:T(8,128)(2,1)} %all-gather.3.cloned.1.call-done, f32[1024]{0:T(1024)S(1)} %bitcast.13, s32[128]{0:T(128)S(1)} %iota_add_fusion), kind=kOutput, calls=%fused_computation.7 | convolution fusion | flops 269090688 | bytes 2364416 | tf_op jit(solution)/shard_map/dot_general | solution.py:12
  77.4 0.7 div.20
  78.1 15.3 %all-to-all-start.2 = ((f32[64,1,2]{2,1,0:T(1,128)}), f32[64,1,2]{2,1,0:T(1,128)S(1)}, u32[]{:S(2)}, u32[]{:S(2)}) async-start(f32[64,1,2]{2,1,0:T(1,128)} %bitcast.4), calls=%async_computation.2 | async-start | bytes 65536 | tf_op jit(solution)/shard_map/all_to_all | solution.py:63
  93.4 9.4 %all-to-all-done.2 = f32[64,1,2]{2,1,0:T(1,128)S(1)} async-done(((f32[64,1,2]{2,1,0:T(1,128)}), f32[64,1,2]{2,1,0:T(1,128)S(1)}, u32[]{:S(2)}, u32[]{:S(2)}) %all-to-all-start.2) | async-done | bytes 544 | tf_op jit(solution)/shard_map/all_to_all | solution.py:63
  102.8 0.5 broadcast.62
  103.3 0.7 reduce.4
  104.0 0.1 reshape.57
  104.2 1.3 %gather_fusion = f32[64]{0:T(128)} fusion(f32[128]{0:T(128)S(1)} %reshape.57, s32[1024]{0:T(1024)S(1)} %pad_clamp_fusion), kind=kCustom, calls=%fused_computation | custom fusion | bytes 768 | tf_op jit(solution)/shard_map/gather | solution.py:64
  (6 shorter events, 0.0 us)
Async XLA Ops:
  6.5 68.2 %all-gather.3.cloned.1.call-start = ((), (), s32[]{:S(2)}) async-start(), calls=%async_computation.3 | async-start | bytes 2359296 | tf_op jit(solution)/shard_map/all_gather | solution.py:54
  41.7 14.2 %all-to-all-start.1 = ((bf16[64,1,2]{2,1,0:T(2,128)(2,1)}), bf16[64,1,2]{2,1,0:T(2,128)(2,1)S(1)}, u32[]{:S(2)}, u32[]{:S(2)}) async-start(bf16[64,1,2]{2,1,0:T(2,128)(2,1)} %all_to_all.17), calls=%async_computation.1 | async-start | bytes 65536 | tf_op jit(solution)/shard_map/all_to_all | solution.py:49
  78.1 24.7 %all-to-all-start.2 = ((f32[64,1,2]{2,1,0:T(1,128)}), f32[64,1,2]{2,1,0:T(1,128)S(1)}, u32[]{:S(2)}, u32[]{:S(2)}) async-start(f32[64,1,2]{2,1,0:T(1,128)} %bitcast.4), calls=%async_computation.2 | async-start | bytes 65536 | tf_op jit(solution)/shard_map/all_to_all | solution.py:63
Sparse Core Ops, SparseCore 0:
  40.1 34.5 all-gather.2
where the time goes:
time: 113 us; the launch traced here: 112 us
  blocking collectives  41.9 us (37%)
  waiting for transfers between devices  23.1 us (20%)
  starting transfers between devices  20 us (18%)
  between operations  13.5 us (12%)
  other arithmetic  5.61 us (5%)
  local copies, waits for them, and re-layouts  5.48 us (5%)
  matrix products  2.65 us (2%)
    all_to_all x1, blocking collectives, shards(): lax.all_to_all(outgoing, 'dp', split_axis=0, concat_axis=0, tiled=True)  27.7 us
    all_to_all x1, starting transfers between devices, shards(): lax.all_to_all(scaled, 'dp', split_axis=0, concat_axis=0, tiled=True)  15.3 us
    all_gather x1, blocking collectives, shards(): piece_flags = lax.all_gather(live_flags, 'group', axis=0, tiled=True)  14.2 us
    all_to_all x1, waiting for transfers between devices, shards(): lax.all_to_all(scaled, 'dp', split_axis=0, concat_axis=0, tiled=True)  9.39 us
    all_to_all x1, waiting for transfers between devices, shards(): lax.all_to_all(occupied, 'dp', split_axis=0, concat_axis=0, tiled=True)  9.39 us
    all_to_all x1, starting transfers between devices, shards(): lax.all_to_all(occupied, 'dp', split_axis=0, concat_axis=0, tiled=True)  4.77 us
    all_gather x1, waiting for transfers between devices, shards(): piece_rows = lax.all_gather(member_rows, 'group', axis=0, tiled=True)  4.32 us
    dot_general x1, matrix products, pair_scores(): lax.dot_general(left_rows, right_rows, (((1,), (1,)), ((), ())), preferre...  2.65 us
  transfers between devices with their start and end apart: 3, of which 3 were waited for; matrix products, arithmetic and copies ran while one was open for 1% of the time, Pallas kernels for 0%

commit v1 on v0

v1 whole, which is shorter than its diff:
```python
import functools
import math

import jax
import jax.numpy as jnp
from jax import lax
from jax.experimental import pallas as pl
from jax.experimental.pallas import tpu as pltpu
from jax.sharding import PartitionSpec as P

MESH = pl.DeviceIdType.MESH
epsilon = 1e-06
Z, X, Y, CORES = 8, 4, 8, 2
SLOTS = Z * Y
PER = 2
ROWS = SLOTS * PER
CHUNKS = 8
LANES = 128
OFFSETS = [(dz, dy) for dz in range(Z) for dy in range(Y)]
GROUP_ORDER = [4, 3, 5, 2, 6, 1, 7, 0]
ROW_ORDER = [4, 3, 5, 2, 6, 1, 7, 0]


def wrap(value, size):
    return lax.rem(value + size, size)


def eye(size):
    return lax.broadcasted_iota(jnp.int32, (size, size), 0) == lax.broadcasted_iota(
        jnp.int32, (size, size), 1
    )


def permutation(tile_major):
    out = lax.broadcasted_iota(jnp.int32, (ROWS, ROWS), 0)
    src = lax.broadcasted_iota(jnp.int32, (ROWS, ROWS), 1)
    wanted = (lax.rem(lax.div(out, 2), 8) * 8 + lax.div(out, 16)) * 2 + lax.rem(out, 2)
    return (src == wanted).astype(jnp.float32).astype(jnp.bfloat16)


def dot_t(left, right):
    return lax.dot_general(
        left, right, (((1,), (1,)), ((), ())), preferred_element_type=jnp.float32
    )


def kernel(
    sharpen,
    x_ref,
    ids_ref,
    out_ref,
    send_buf,
    raw,
    blocks,
    part_send,
    part_recv,
    ret_src,
    ret,
    a2a_send,
    a2a_recv,
    fwd_send,
    fwd_recv,
    part_ssem,
    part_rsem,
    ret_ssem,
    ret_rsem,
):
    dp, y = lax.axis_index("dp"), lax.axis_index("group")
    z = lax.div(dp, X * CORES)
    x = lax.rem(lax.div(dp, CORES), X)
    core = lax.rem(dp, CORES)
    other = 1 - core
    right, left = wrap(x + 1, X), wrap(x - 1, X)

    def device(zz, xx, cc, yy):
        return ((zz * X + xx) * CORES + cc, yy)

    def plane(dz, dy):
        return device(wrap(z + dz, Z), x, core, wrap(y + dy, Y))

    partner = device(z, x, other, y)
    swap = lax.div(right, 2)
    own_swap = lax.div(x, 2)
    to_right = device(z, right, core + swap * (1 - 2 * core), y)
    to_left = device(z, left, core, y)
    from_right = device(z, right, core, y)
    from_left = device(z, left, core + own_swap * (1 - 2 * core), y)

    barrier = pltpu.get_barrier_semaphore()
    for dz, dy in OFFSETS[1:]:
        pl.semaphore_signal(barrier, inc=1, device_id=plane(dz, dy), device_id_type=MESH)
    near = [partner] + [device(z, xx, cc, y) for xx in (left, right) for cc in (0, 1)]
    for target in near:
        pl.semaphore_signal(barrier, inc=1, device_id=target, device_id_type=MESH)

    docs = x_ref.shape[0]
    widened = x_ref[...].astype(jnp.float32)
    normed = (
        widened / jnp.sqrt(jnp.sum(widened * widened, axis=1, keepdims=True) + epsilon)
    ).astype(jnp.bfloat16)

    ids_row = ids_ref[...]
    ids_col = jnp.sum(jnp.where(eye(docs), ids_row, 0), axis=1, keepdims=True)
    earlier = lax.broadcasted_iota(jnp.int32, (docs, docs), 0) < lax.broadcasted_iota(
        jnp.int32, (docs, docs), 1
    )
    within = jnp.sum(jnp.where((ids_col == ids_row) & earlier, 1, 0), axis=0, keepdims=True)
    slot_row = lax.broadcasted_iota(jnp.int32, (ROWS, 1), 0)
    owner = (
        lax.rem(z + lax.div(slot_row, 2 * Y), Z) * Y
        + lax.rem(y + lax.rem(lax.div(slot_row, 2), Y), Y)
    )
    chosen = (owner == ids_row) & (lax.rem(slot_row, 2) == within)
    onehot = jnp.where(chosen, 1.0, 0.0)
    empty = jnp.sum(onehot, axis=1, keepdims=True) == 0.0

    packed = jnp.dot(onehot.astype(jnp.bfloat16), normed, preferred_element_type=jnp.float32)
    first = lax.broadcasted_iota(jnp.int32, packed.shape, 1) == 0
    packed = jnp.where(empty & first, 2.0, packed).astype(jnp.bfloat16)
    perm = permutation(True)
    stacked = jnp.concatenate(
        [
            jnp.concatenate(
                [packed[16 * g : 16 * g + 16, LANES * k : LANES * k + LANES] for k in range(CHUNKS)],
                axis=0,
            )
            for g in range(Z)
        ],
        axis=1,
    )
    tiles = jnp.dot(perm, stacked, preferred_element_type=jnp.float32).astype(jnp.bfloat16)
    for g in range(Z):
        for dy in range(Y):
            tile = tiles[16 * dy : 16 * dy + 16, LANES * g : LANES * g + LANES]
            if g == 0 and dy == 0:
                raw[0, 0] = tile
            else:
                send_buf[g * Y + dy] = tile

    pl.semaphore_wait(barrier, SLOTS - 1 + len(near))

    for dz in GROUP_ORDER:
        for dy in ROW_ORDER:
            if (dz, dy) == (0, 0):
                continue
            slot = dz * Y + dy
            pltpu.make_async_remote_copy(
                src_ref=send_buf.at[slot],
                dst_ref=raw.at[0, slot],
                send_sem=a2a_send,
                recv_sem=a2a_recv.at[dz],
                device_id=plane(dz, dy),
                device_id_type=MESH,
            ).start()

    def convert(which, row, g):
        got = raw[which, g * Y : (g + 1) * Y].reshape(ROWS, LANES)
        turned = jnp.dot(perm, got, preferred_element_type=jnp.float32).astype(jnp.bfloat16)
        for k in range(CHUNKS):
            blocks[row + 16 * g : row + 16 * g + 16, LANES * k : LANES * k + LANES] = turned[
                16 * k : 16 * k + 16
            ]

    starts = (ROWS, 2 * ROWS, 0, 3 * ROWS)
    targets = (None, partner, to_left, to_right)

    def forward(which, g):
        return pltpu.make_async_remote_copy(
            src_ref=raw.at[0, pl.ds(g * Y, Y)],
            dst_ref=raw.at[which, pl.ds(g * Y, Y)],
            send_sem=fwd_send.at[which - 1, g],
            recv_sem=fwd_recv.at[which - 1, g],
            device_id=targets[which],
            device_id_type=MESH,
        )

    for g in GROUP_ORDER:
        skip = 1 if g == 0 else 0
        arrived = raw.at[0, pl.ds(g * Y + skip, Y - skip)]
        pltpu.make_async_copy(arrived, arrived, a2a_recv.at[g]).wait()
        for which in (3, 2, 1):
            forward(which, g).start()
        convert(0, starts[0], g)
    for g in GROUP_ORDER:
        for which in (1, 2, 3):
            forward(which, g).wait_recv()
            convert(which, starts[which], g)

    from_r, own, mate, from_l = (pl.ds(start, ROWS) for start in (0, ROWS, 2 * ROWS, 3 * ROWS))

    def column_sums(rows, columns, diagonal_at=None):
        source = blocks[rows, :]
        scores = dot_t(source, blocks[columns, :])
        keep = source[:, 0:1].astype(jnp.float32) < 1.5
        if diagonal_at is not None:
            keep = keep & (
                lax.broadcasted_iota(jnp.int32, scores.shape, 0)
                != lax.broadcasted_iota(jnp.int32, scores.shape, 1) + diagonal_at
            )
        return jnp.sum(
            jnp.where(keep, jnp.exp(scores * sharpen), 0.0), axis=0, keepdims=True
        )

    part_send[0] = column_sums(pl.ds(ROWS, 3 * ROWS), from_r)
    both = column_sums(from_r, pl.ds(2 * ROWS, 2 * ROWS))
    part_send[1] = both[:, :ROWS]
    part_send[2] = both[:, ROWS:]

    def part(which):
        return pltpu.make_async_remote_copy(
            src_ref=part_send.at[which],
            dst_ref=part_recv.at[which],
            send_sem=part_ssem.at[which],
            recv_sem=part_rsem.at[which],
            device_id=(from_right, partner, from_left)[which],
            device_id_type=MESH,
        )

    for which in range(3):
        part(which).start()
    total = column_sums(pl.ds(0, 3 * ROWS), own, diagonal_at=ROWS)
    for which in range(3):
        part(which).wait_recv()
        total = total + part_recv[which]
    total = total * (1.0 / (docs * Y))
    ret_src[0] = total
    ret[0] = total
    for dz in GROUP_ORDER:
        for dy in ROW_ORDER:
            if (dz, dy) == (0, 0):
                continue
            pltpu.make_async_remote_copy(
                src_ref=ret_src.at[0],
                dst_ref=ret.at[dz * Y + dy],
                send_sem=ret_ssem,
                recv_sem=ret_rsem,
                device_id=plane(-dz, -dy),
                device_id_type=MESH,
            ).start()

    sent = send_buf.at[pl.ds(1, SLOTS - 1)]
    pltpu.make_async_copy(sent, sent, a2a_send).wait()
    for g in range(Z):
        for which in (1, 2, 3):
            forward(which, g).wait_send()
    for which in range(3):
        part(which).wait_send()
    back = ret.at[pl.ds(1, SLOTS - 1)]
    pltpu.make_async_copy(back, back, ret_rsem).wait()

    lane = lax.broadcasted_iota(jnp.int32, (SLOTS, 1, LANES), 2)
    slot = lax.broadcasted_iota(jnp.int32, (SLOTS, 1, LANES), 0)
    mine = jnp.sum(jnp.where(lax.div(lane, 2) == slot, ret[...], 0.0), axis=0)
    column = jnp.sum(jnp.where(eye(ROWS), mine, 0.0), axis=1, keepdims=True)
    out_ref[...] = jnp.sum(jnp.where(chosen, column, 0.0), axis=0, keepdims=True)
    pltpu.make_async_copy(back, back, ret_ssem).wait()


def shards(embeddings, cluster_ids):
    docs, width = embeddings.shape
    vmem = pl.BlockSpec(memory_space=pltpu.VMEM)
    bf16, f32 = jnp.bfloat16, jnp.float32
    out = pl.pallas_call(
        functools.partial(kernel, math.sqrt(width)),
        out_shape=jax.ShapeDtypeStruct((1, docs), f32),
        in_specs=[vmem, vmem],
        out_specs=vmem,
        scratch_shapes=[
            pltpu.VMEM((SLOTS, 16, LANES), bf16),
            pltpu.VMEM((4, SLOTS, 16, LANES), bf16),
            pltpu.VMEM((4 * ROWS, width), bf16),
            pltpu.VMEM((3, 1, LANES), f32),
            pltpu.VMEM((3, 1, LANES), f32),
            pltpu.VMEM((1, 1, LANES), f32),
            pltpu.VMEM((SLOTS, 1, LANES), f32),
            pltpu.SemaphoreType.DMA,
            pltpu.SemaphoreType.DMA((Z,)),
            pltpu.SemaphoreType.DMA((3, Z)),
            pltpu.SemaphoreType.DMA((3, Z)),
            pltpu.SemaphoreType.DMA((3,)),
            pltpu.SemaphoreType.DMA((3,)),
            pltpu.SemaphoreType.DMA,
            pltpu.SemaphoreType.DMA,
        ],
        compiler_params=pltpu.CompilerParams(collective_id=0, has_side_effects=True),
    )(embeddings, cluster_ids.reshape(1, docs))
    return out.reshape(docs)


def solution(mesh):
    placed = (P(("dp", "group"), None), P(("dp", "group"), None))
    return jax.shard_map(
        shards, mesh=mesh, in_specs=placed, out_specs=P(("dp", "group")), check_vma=False
    )
```

time: 113 us -> 44.2 us (0.39)
  Pallas kernels: 0 us -> 42.6 us
  blocking collectives: 41.9 us -> 0 us
  waiting for transfers between devices: 23.1 us -> 0 us
  starting transfers between devices: 20 us -> 0 us
  between operations: 13.5 us -> 0.02 us
  other arithmetic: 5.61 us -> 0 us
  local copies, waits for them, and re-layouts: 5.48 us -> 1.1 us
  matrix products: 2.65 us -> 0 us
    pallas_call x0 -> x1, Pallas kernels: none -> 42.6 us  [shards(): pl.pallas_call(functools.partial(kernel, math.sqrt(width)), out_shape=jax...]
    all_to_all x1 -> x0, blocking collectives: 27.7 us -> none  [shards(): lax.all_to_all(outgoing, 'dp', split_axis=0, concat_axis=0, tiled=True)]
    all_to_all x2 -> x0, starting transfers between devices: 20 us -> none  [the longest x1 15.3 us: shards(): lax.all_to_all(scaled, 'dp', split_axis=0, concat_axis=0, tiled=True)]
    all_to_all x2 -> x0, waiting for transfers between devices: 18.8 us -> none  [the longest x1 9.39 us: shards(): lax.all_to_all(scaled, 'dp', split_axis=0, concat_axis=0, tiled=True)]
    all_gather x1 -> x0, blocking collectives: 14.2 us -> none  [shards(): piece_flags = lax.all_gather(live_flags, 'group', axis=0, tiled=True)]
    all_gather x1 -> x0, waiting for transfers between devices: 4.32 us -> none  [shards(): piece_rows = lax.all_gather(member_rows, 'group', axis=0, tiled=True)]
    dot_general x1 -> x0, matrix products: 2.65 us -> none  [pair_scores(): lax.dot_general(left_rows, right_rows, (((1,), (1,)), ((), ())), preferre...]
    reduce_sum x2 -> x0, other arithmetic: 1.86 us -> none  [the longest x1 1.03 us: shards(): jnp.sum(widened * widened, axis=1, keepdims=True) + epsilon]
  transfers between devices with their start and end apart: 3 -> 0, of which waited for: 3 -> 0; matrix products, arithmetic and copies ran while one was open for 1% -> 0% of each run, Pallas kernels for 0% -> 0%
where the time goes in v1:
time: 44.2 us; the launch traced here: 43.7 us
  Pallas kernels  42.6 us (96%)
  local copies, waits for them, and re-layouts  1.1 us (2%)
    pallas_call x1, Pallas kernels, shards(): pl.pallas_call(functools.partial(kernel, math.sqrt(width)), out_shape=jax...  42.6 us
    unnamed x3, local copies, waits for them, and re-layouts  1.1 us

profile of v1, /device:TPU:1, one launch (start us, length us, event | category | flops | bytes accessed | tf_op | source)
XLA Modules:
  0.0 43.7 jit_solution(7412634996972670312)
XLA Ops:
  0.0 42.6 %shard_map.28 = f32[1,64]{1,0:T(1,128)} custom-call(bf16[64,1024]{1,0:T(8,128)(2,1)} %x_ref.1, s32[1,64]{1,0:T(1,128)} %bitcast.2), custom_call_target="tpu_custom_call" | custom-call | tf_op jit(solution)/shard_map/pallas_call | solution.py:263
  42.6 0.0 copy-start
  42.6 0.6 %copy-done = f32[1,64]{1,0:T(1,128)S(1)} copy-done((f32[1,64]{1,0:T(1,128)S(1)}, f32[1,64]{1,0:T(1,128)}, u32[]{:S(2)}) %copy-start) | copy-done | bytes 280
  43.2 0.5 %copy.4 = f32[64]{0:T(128)} copy(f32[64]{0:T(128)S(1)} %bitcast.3) | data formatting | bytes 512
Async XLA Ops:
  42.6 0.6 %copy-start = (f32[1,64]{1,0:T(1,128)S(1)}, f32[1,64]{1,0:T(1,128)}, u32[]{:S(2)}) copy-start(f32[1,64]{1,0:T(1,128)} %shard_map.28) | copy-start | bytes 772

commit v2 on v1

--- a/solution.py
+++ b/solution.py
@@ -16,9 +16,15 @@
 ROWS = SLOTS * PER
 CHUNKS = 8
 LANES = 128
-OFFSETS = [(dz, dy) for dz in range(Z) for dy in range(Y)]
-GROUP_ORDER = [4, 3, 5, 2, 6, 1, 7, 0]
-ROW_ORDER = [4, 3, 5, 2, 6, 1, 7, 0]
+
+
+def hops(offset):
+    dz, dy = offset
+    return min(dz, Z - dz) + min(dy, Y - dy)
+
+
+OFFSETS = sorted([(dz, dy) for dz in range(Z) for dy in range(Y)], key=lambda at: (hops(at), at))
+GROUPS = SLOTS // 8
 
 
 def wrap(value, size):
@@ -46,8 +52,8 @@
 
 def kernel(
     sharpen,
-    x_ref,
-    ids_ref,
+    x_hbm,
+    ids_hbm,
     out_ref,
     send_buf,
     raw,
@@ -64,6 +70,9 @@
     part_rsem,
     ret_ssem,
     ret_rsem,
+    x_ref,
+    ids_ref,
+    in_sem,
 ):
     dp, y = lax.axis_index("dp"), lax.axis_index("group")
     z = lax.div(dp, X * CORES)
@@ -86,12 +95,19 @@
     from_right = device(z, right, core, y)
     from_left = device(z, left, core + own_swap * (1 - 2 * core), y)
 
+    load_x = pltpu.make_async_copy(x_hbm, x_ref, in_sem.at[0])
+    load_ids = pltpu.make_async_copy(ids_hbm, ids_ref, in_sem.at[1])
+    load_x.start()
+    load_ids.start()
     barrier = pltpu.get_barrier_semaphore()
-    for dz, dy in OFFSETS[1:]:
+    for dz, dy in OFFSETS[:0:-1]:
         pl.semaphore_signal(barrier, inc=1, device_id=plane(dz, dy), device_id_type=MESH)
     near = [partner] + [device(z, xx, cc, y) for xx in (left, right) for cc in (0, 1)]
     for target in near:
         pl.semaphore_signal(barrier, inc=1, device_id=target, device_id_type=MESH)
+
+    load_x.wait()
+    load_ids.wait()
 
     docs = x_ref.shape[0]
     widened = x_ref[...].astype(jnp.float32)
@@ -106,10 +122,12 @@
     )
     within = jnp.sum(jnp.where((ids_col == ids_row) & earlier, 1, 0), axis=0, keepdims=True)
     slot_row = lax.broadcasted_iota(jnp.int32, (ROWS, 1), 0)
-    owner = (
-        lax.rem(z + lax.div(slot_row, 2 * Y), Z) * Y
-        + lax.rem(y + lax.rem(lax.div(slot_row, 2), Y), Y)
-    )
+    slot = lax.div(slot_row, 2)
+    owner_z, owner_y = z + jnp.zeros_like(slot), y + jnp.zeros_like(slot)
+    for k, (dz, dy) in enumerate(OFFSETS):
+        owner_z = owner_z + jnp.where(slot == k, dz, 0)
+        owner_y = owner_y + jnp.where(slot == k, dy, 0)
+    owner = lax.rem(owner_z, Z) * Y + lax.rem(owner_y, Y)
     chosen = (owner == ids_row) & (lax.rem(slot_row, 2) == within)
     onehot = jnp.where(chosen, 1.0, 0.0)
     empty = jnp.sum(onehot, axis=1, keepdims=True) == 0.0
@@ -124,37 +142,33 @@
                 [packed[16 * g : 16 * g + 16, LANES * k : LANES * k + LANES] for k in range(CHUNKS)],
                 axis=0,
             )
-            for g in range(Z)
+            for g in range(GROUPS)
         ],
         axis=1,
     )
     tiles = jnp.dot(perm, stacked, preferred_element_type=jnp.float32).astype(jnp.bfloat16)
-    for g in range(Z):
-        for dy in range(Y):
-            tile = tiles[16 * dy : 16 * dy + 16, LANES * g : LANES * g + LANES]
-            if g == 0 and dy == 0:
-                raw[0, 0] = tile
-            else:
-                send_buf[g * Y + dy] = tile
+    for k in range(SLOTS):
+        g, row = k // 8, 16 * (k % 8)
+        tile = tiles[row : row + 16, LANES * g : LANES * g + LANES]
+        if k == 0:
+            raw[0, 0] = tile
+        else:
+            send_buf[k] = tile
 
     pl.semaphore_wait(barrier, SLOTS - 1 + len(near))
 
-    for dz in GROUP_ORDER:
-        for dy in ROW_ORDER:
-            if (dz, dy) == (0, 0):
-                continue
-            slot = dz * Y + dy
-            pltpu.make_async_remote_copy(
-                src_ref=send_buf.at[slot],
-                dst_ref=raw.at[0, slot],
-                send_sem=a2a_send,
-                recv_sem=a2a_recv.at[dz],
-                device_id=plane(dz, dy),
-                device_id_type=MESH,
-            ).start()
+    for k, (dz, dy) in list(enumerate(OFFSETS))[1:]:
+        pltpu.make_async_remote_copy(
+            src_ref=send_buf.at[k],
+            dst_ref=raw.at[0, k],
+            send_sem=a2a_send,
+            recv_sem=a2a_recv.at[k // 8],
+            device_id=plane(dz, dy),
+            device_id_type=MESH,
+        ).start()
 
     def convert(which, row, g):
-        got = raw[which, g * Y : (g + 1) * Y].reshape(ROWS, LANES)
+        got = raw[which, 8 * g : 8 * g + 8].reshape(ROWS, LANES)
         turned = jnp.dot(perm, got, preferred_element_type=jnp.float32).astype(jnp.bfloat16)
         for k in range(CHUNKS):
             blocks[row + 16 * g : row + 16 * g + 16, LANES * k : LANES * k + LANES] = turned[
@@ -166,22 +180,22 @@
 
     def forward(which, g):
         return pltpu.make_async_remote_copy(
-            src_ref=raw.at[0, pl.ds(g * Y, Y)],
-            dst_ref=raw.at[which, pl.ds(g * Y, Y)],
+            src_ref=raw.at[0, pl.ds(8 * g, 8)],
+            dst_ref=raw.at[which, pl.ds(8 * g, 8)],
             send_sem=fwd_send.at[which - 1, g],
             recv_sem=fwd_recv.at[which - 1, g],
             device_id=targets[which],
             device_id_type=MESH,
         )
 
-    for g in GROUP_ORDER:
+    for g in range(GROUPS):
         skip = 1 if g == 0 else 0
-        arrived = raw.at[0, pl.ds(g * Y + skip, Y - skip)]
+        arrived = raw.at[0, pl.ds(8 * g + skip, 8 - skip)]
         pltpu.make_async_copy(arrived, arrived, a2a_recv.at[g]).wait()
         for which in (3, 2, 1):
             forward(which, g).start()
         convert(0, starts[0], g)
-    for g in GROUP_ORDER:
+    for g in range(GROUPS):
         for which in (1, 2, 3):
             forward(which, g).wait_recv()
             convert(which, starts[which], g)
@@ -222,25 +236,21 @@
     for which in range(3):
         part(which).wait_recv()
         total = total + part_recv[which]
-    total = total * (1.0 / (docs * Y))
     ret_src[0] = total
     ret[0] = total
-    for dz in GROUP_ORDER:
-        for dy in ROW_ORDER:
-            if (dz, dy) == (0, 0):
-                continue
-            pltpu.make_async_remote_copy(
-                src_ref=ret_src.at[0],
-                dst_ref=ret.at[dz * Y + dy],
-                send_sem=ret_ssem,
-                recv_sem=ret_rsem,
-                device_id=plane(-dz, -dy),
-                device_id_type=MESH,
-            ).start()
+    for k, (dz, dy) in list(enumerate(OFFSETS))[:0:-1]:
+        pltpu.make_async_remote_copy(
+            src_ref=ret_src.at[0],
+            dst_ref=ret.at[k],
+            send_sem=ret_ssem,
+            recv_sem=ret_rsem,
+            device_id=plane(-dz, -dy),
+            device_id_type=MESH,
+        ).start()
 
     sent = send_buf.at[pl.ds(1, SLOTS - 1)]
     pltpu.make_async_copy(sent, sent, a2a_send).wait()
-    for g in range(Z):
+    for g in range(GROUPS):
         for which in (1, 2, 3):
             forward(which, g).wait_send()
     for which in range(3):
@@ -249,8 +259,8 @@
     pltpu.make_async_copy(back, back, ret_rsem).wait()
 
     lane = lax.broadcasted_iota(jnp.int32, (SLOTS, 1, LANES), 2)
-    slot = lax.broadcasted_iota(jnp.int32, (SLOTS, 1, LANES), 0)
-    mine = jnp.sum(jnp.where(lax.div(lane, 2) == slot, ret[...], 0.0), axis=0)
+    at = lax.broadcasted_iota(jnp.int32, (SLOTS, 1, LANES), 0)
+    mine = jnp.sum(jnp.where(lax.div(lane, 2) == at, ret[...], 0.0), axis=0)
     column = jnp.sum(jnp.where(eye(ROWS), mine, 0.0), axis=1, keepdims=True)
     out_ref[...] = jnp.sum(jnp.where(chosen, column, 0.0), axis=0, keepdims=True)
     pltpu.make_async_copy(back, back, ret_ssem).wait()
@@ -263,7 +273,7 @@
     out = pl.pallas_call(
         functools.partial(kernel, math.sqrt(width)),
         out_shape=jax.ShapeDtypeStruct((1, docs), f32),
-        in_specs=[vmem, vmem],
+        in_specs=[pl.BlockSpec(memory_space=pl.ANY)] * 2,
         out_specs=vmem,
         scratch_shapes=[
             pltpu.VMEM((SLOTS, 16, LANES), bf16),
@@ -274,17 +284,20 @@
             pltpu.VMEM((1, 1, LANES), f32),
             pltpu.VMEM((SLOTS, 1, LANES), f32),
             pltpu.SemaphoreType.DMA,
-            pltpu.SemaphoreType.DMA((Z,)),
-            pltpu.SemaphoreType.DMA((3, Z)),
-            pltpu.SemaphoreType.DMA((3, Z)),
+            pltpu.SemaphoreType.DMA((GROUPS,)),
+            pltpu.SemaphoreType.DMA((3, GROUPS)),
+            pltpu.SemaphoreType.DMA((3, GROUPS)),
             pltpu.SemaphoreType.DMA((3,)),
             pltpu.SemaphoreType.DMA((3,)),
             pltpu.SemaphoreType.DMA,
             pltpu.SemaphoreType.DMA,
+            pltpu.VMEM((docs, width), bf16),
+            pltpu.VMEM((1, docs), jnp.int32),
+            pltpu.SemaphoreType.DMA((2,)),
         ],
         compiler_params=pltpu.CompilerParams(collective_id=0, has_side_effects=True),
     )(embeddings, cluster_ids.reshape(1, docs))
-    return out.reshape(docs)
+    return out.reshape(docs) * (1.0 / (docs * Y))
 
 
 def solution(mesh):

time: 44.2 us -> 43.9 us (level)
  the two profiles are of different devices: /device:TPU:1 before, /device:TPU:8 now
where the time goes in v2:
time: 43.9 us; the launch traced here: 43.8 us
  Pallas kernels  42.6 us (97%)
  other arithmetic  1.19 us (3%)
    pallas_call x1, Pallas kernels, shards(): pl.pallas_call(functools.partial(kernel, math.sqrt(width)), out_shape=jax...  42.6 us
    mul x1, other arithmetic, shards(): return out.reshape(docs) * (1.0 / (docs * Y))  1.19 us

profile of v2, /device:TPU:8, one launch (start us, length us, event | category | flops | bytes accessed | tf_op | source)
XLA Modules:
  0.0 43.8 jit_solution(16709198301696376795)
XLA Ops:
  0.0 42.6 %shard_map.28 = f32[1,64]{1,0:T(1,128)} custom-call(bf16[64,1024]{1,0:T(8,128)(2,1)} %x_hbm.1, s32[1,64]{1,0:T(1,128)} %bitcast.3), custom_call_target="tpu_custom_call" | custom-call | tf_op jit(solution)/shard_map/pallas_call | solution.py:273
  42.6 1.2 %multiply_bitcast_fusion = f32[64]{0:T(128)} fusion(f32[1,64]{1,0:T(1,128)} %shard_map.28), kind=kLoop, calls=%fused_computation | loop fusion | flops 64 | bytes 512 | tf_op jit(solution)/shard_map/mul | solution.py:300

commit v3 on v2

--- a/solution.py
+++ b/solution.py
@@ -17,14 +17,17 @@
 CHUNKS = 8
 LANES = 128
 
-
-def hops(offset):
-    dz, dy = offset
-    return min(dz, Z - dz) + min(dy, Y - dy)
-
-
-OFFSETS = sorted([(dz, dy) for dz in range(Z) for dy in range(Y)], key=lambda at: (hops(at), at))
-GROUPS = SLOTS // 8
+RING = 8
+NEAREST = [0, 1, 7, 2, 6, 3, 5, 4]
+PIECES = [(0, 1), (1, 8)]
+GROUPS = SLOTS // RING
+FIRST_ORDER = [7, 6, 5, 4, 3, 2, 1]
+SECOND_ORDER = [1, 2, 3, 4, 5, 6, 7]
+
+
+def offset_of(place):
+    half = lax.div(place + 1, 2)
+    return jnp.where(lax.rem(place, 2) == 1, half, lax.rem(RING - half, RING))
 
 
 def wrap(value, size):
@@ -56,14 +59,17 @@
     ids_hbm,
     out_ref,
     send_buf,
+    middle,
     raw,
     blocks,
     part_send,
     part_recv,
     ret_src,
     ret,
-    a2a_send,
-    a2a_recv,
+    one_send,
+    one_recv,
+    two_send,
+    two_recv,
     fwd_send,
     fwd_recv,
     part_ssem,
@@ -84,7 +90,9 @@
     def device(zz, xx, cc, yy):
         return ((zz * X + xx) * CORES + cc, yy)
 
-    def plane(dz, dy):
+    def plane(first, second):
+        dz = second + core * (first - second)
+        dy = first + core * (second - first)
         return device(wrap(z + dz, Z), x, core, wrap(y + dy, Y))
 
     partner = device(z, x, other, y)
@@ -100,8 +108,9 @@
     load_x.start()
     load_ids.start()
     barrier = pltpu.get_barrier_semaphore()
-    for dz, dy in OFFSETS[:0:-1]:
-        pl.semaphore_signal(barrier, inc=1, device_id=plane(dz, dy), device_id_type=MESH)
+    for away in NEAREST[:0:-1]:
+        for target in (plane(away, 0), plane(0, away)):
+            pl.semaphore_signal(barrier, inc=1, device_id=target, device_id_type=MESH)
     near = [partner] + [device(z, xx, cc, y) for xx in (left, right) for cc in (0, 1)]
     for target in near:
         pl.semaphore_signal(barrier, inc=1, device_id=target, device_id_type=MESH)
@@ -123,11 +132,10 @@
     within = jnp.sum(jnp.where((ids_col == ids_row) & earlier, 1, 0), axis=0, keepdims=True)
     slot_row = lax.broadcasted_iota(jnp.int32, (ROWS, 1), 0)
     slot = lax.div(slot_row, 2)
-    owner_z, owner_y = z + jnp.zeros_like(slot), y + jnp.zeros_like(slot)
-    for k, (dz, dy) in enumerate(OFFSETS):
-        owner_z = owner_z + jnp.where(slot == k, dz, 0)
-        owner_y = owner_y + jnp.where(slot == k, dy, 0)
-    owner = lax.rem(owner_z, Z) * Y + lax.rem(owner_y, Y)
+    first, second = offset_of(lax.rem(slot, RING)), offset_of(lax.div(slot, RING))
+    owner_z = lax.rem(z + second + core * (first - second), Z)
+    owner_y = lax.rem(y + first + core * (second - first), Y)
+    owner = owner_z * Y + owner_y
     chosen = (owner == ids_row) & (lax.rem(slot_row, 2) == within)
     onehot = jnp.where(chosen, 1.0, 0.0)
     empty = jnp.sum(onehot, axis=1, keepdims=True) == 0.0
@@ -150,25 +158,45 @@
     for k in range(SLOTS):
         g, row = k // 8, 16 * (k % 8)
         tile = tiles[row : row + 16, LANES * g : LANES * g + LANES]
-        if k == 0:
-            raw[0, 0] = tile
+        if k % RING == 0:
+            middle[g, 0] = tile
         else:
-            send_buf[k] = tile
-
-    pl.semaphore_wait(barrier, SLOTS - 1 + len(near))
-
-    for k, (dz, dy) in list(enumerate(OFFSETS))[1:]:
-        pltpu.make_async_remote_copy(
-            src_ref=send_buf.at[k],
-            dst_ref=raw.at[0, k],
-            send_sem=a2a_send,
-            recv_sem=a2a_recv.at[k // 8],
-            device_id=plane(dz, dy),
-            device_id_type=MESH,
-        ).start()
+            send_buf[k % RING, g] = tile
+
+    pl.semaphore_wait(barrier, 2 * (RING - 1) + len(near))
+
+    def along_first(a):
+        return pltpu.make_async_remote_copy(
+            src_ref=send_buf.at[a],
+            dst_ref=middle.at[pl.ds(0, RING), a],
+            send_sem=one_send,
+            recv_sem=one_recv.at[a],
+            device_id=plane(NEAREST[a], 0),
+            device_id_type=MESH,
+        )
+
+    def along_second(b, piece):
+        low, high = PIECES[piece]
+        return pltpu.make_async_remote_copy(
+            src_ref=middle.at[b, pl.ds(low, high - low)],
+            dst_ref=raw.at[0, pl.ds(b * RING + low, high - low)],
+            send_sem=two_send,
+            recv_sem=two_recv.at[b, piece],
+            device_id=plane(0, NEAREST[b]),
+            device_id_type=MESH,
+        )
+
+    for a in FIRST_ORDER:
+        along_first(a).start()
+    for piece, (low, high) in enumerate(PIECES):
+        for a in range(max(low, 1), high):
+            along_first(a).wait_recv()
+        for b in SECOND_ORDER:
+            along_second(b, piece).start()
 
     def convert(which, row, g):
-        got = raw[which, 8 * g : 8 * g + 8].reshape(ROWS, LANES)
+        got = middle[0] if which == 0 and g == 0 else raw[which, 8 * g : 8 * g + 8]
+        got = got.reshape(ROWS, LANES)
         turned = jnp.dot(perm, got, preferred_element_type=jnp.float32).astype(jnp.bfloat16)
         for k in range(CHUNKS):
             blocks[row + 16 * g : row + 16 * g + 16, LANES * k : LANES * k + LANES] = turned[
@@ -180,7 +208,7 @@
 
     def forward(which, g):
         return pltpu.make_async_remote_copy(
-            src_ref=raw.at[0, pl.ds(8 * g, 8)],
+            src_ref=middle.at[0] if g == 0 else raw.at[0, pl.ds(8 * g, 8)],
             dst_ref=raw.at[which, pl.ds(8 * g, 8)],
             send_sem=fwd_send.at[which - 1, g],
             recv_sem=fwd_recv.at[which - 1, g],
@@ -189,9 +217,9 @@
         )
 
     for g in range(GROUPS):
-        skip = 1 if g == 0 else 0
-        arrived = raw.at[0, pl.ds(8 * g + skip, 8 - skip)]
-        pltpu.make_async_copy(arrived, arrived, a2a_recv.at[g]).wait()
+        if g > 0:
+            for piece in range(len(PIECES)):
+                along_second(g, piece).wait_recv()
         for which in (3, 2, 1):
             forward(which, g).start()
         convert(0, starts[0], g)
@@ -238,18 +266,19 @@
         total = total + part_recv[which]
     ret_src[0] = total
     ret[0] = total
-    for k, (dz, dy) in list(enumerate(OFFSETS))[:0:-1]:
+    for k in range(SLOTS - 1, 0, -1):
         pltpu.make_async_remote_copy(
             src_ref=ret_src.at[0],
             dst_ref=ret.at[k],
             send_sem=ret_ssem,
             recv_sem=ret_rsem,
-            device_id=plane(-dz, -dy),
+            device_id=plane(-NEAREST[k % RING], -NEAREST[k // RING]),
             device_id_type=MESH,
         ).start()
 
-    sent = send_buf.at[pl.ds(1, SLOTS - 1)]
-    pltpu.make_async_copy(sent, sent, a2a_send).wait()
+    for sent, sem in ((send_buf, one_send), (middle, two_send)):
+        most = sent.at[pl.ds(1, RING - 1)]
+        pltpu.make_async_copy(most, most, sem).wait()
     for g in range(GROUPS):
         for which in (1, 2, 3):
             forward(which, g).wait_send()
@@ -276,7 +305,8 @@
         in_specs=[pl.BlockSpec(memory_space=pl.ANY)] * 2,
         out_specs=vmem,
         scratch_shapes=[
-            pltpu.VMEM((SLOTS, 16, LANES), bf16),
+            pltpu.VMEM((RING, RING, 16, LANES), bf16),
+            pltpu.VMEM((RING, RING, 16, LANES), bf16),
             pltpu.VMEM((4, SLOTS, 16, LANES), bf16),
             pltpu.VMEM((4 * ROWS, width), bf16),
             pltpu.VMEM((3, 1, LANES), f32),
@@ -284,7 +314,9 @@
             pltpu.VMEM((1, 1, LANES), f32),
             pltpu.VMEM((SLOTS, 1, LANES), f32),
             pltpu.SemaphoreType.DMA,
-            pltpu.SemaphoreType.DMA((GROUPS,)),
+            pltpu.SemaphoreType.DMA((RING,)),
+            pltpu.SemaphoreType.DMA,
+            pltpu.SemaphoreType.DMA((RING, len(PIECES))),
             pltpu.SemaphoreType.DMA((3, GROUPS)),
             pltpu.SemaphoreType.DMA((3, GROUPS)),
             pltpu.SemaphoreType.DMA((3,)),

time: 43.9 us -> 43.1 us (0.982)
  the two profiles are of different devices: /device:TPU:8 before, /device:TPU:1 now
where the time goes in v3:
time: 43.1 us; the launch traced here: 42.5 us
  Pallas kernels  41.3 us (96%)
  other arithmetic  1.19 us (3%)
    pallas_call x1, Pallas kernels, shards(): pl.pallas_call(functools.partial(kernel, math.sqrt(width)), out_shape=jax...  41.3 us
    mul x1, other arithmetic, shards(): return out.reshape(docs) * (1.0 / (docs * Y))  1.19 us

profile of v3, /device:TPU:1, one launch (start us, length us, event | category | flops | bytes accessed | tf_op | source)
XLA Modules:
  0.0 42.5 jit_solution(13959883699160167056)
XLA Ops:
  0.0 41.3 %shard_map.28 = f32[1,64]{1,0:T(1,128)} custom-call(bf16[64,1024]{1,0:T(8,128)(2,1)} %x_hbm.1, s32[1,64]{1,0:T(1,128)} %bitcast.3), custom_call_target="tpu_custom_call" | custom-call | tf_op jit(solution)/shard_map/pallas_call | solution.py:302
  41.3 1.2 %multiply_bitcast_fusion = f32[64]{0:T(128)} fusion(f32[1,64]{1,0:T(1,128)} %shard_map.28), kind=kLoop, calls=%fused_computation | loop fusion | flops 64 | bytes 512 | tf_op jit(solution)/shard_map/mul | solution.py:332

commit v4 on v3

--- a/solution.py
+++ b/solution.py
@@ -301,7 +301,7 @@
     bf16, f32 = jnp.bfloat16, jnp.float32
     out = pl.pallas_call(
         functools.partial(kernel, math.sqrt(width)),
-        out_shape=jax.ShapeDtypeStruct((1, docs), f32),
+        out_shape=pltpu.VMEM((1, docs), f32),
         in_specs=[pl.BlockSpec(memory_space=pl.ANY)] * 2,
         out_specs=vmem,
         scratch_shapes=[

time: 43.1 us -> 41.9 us (0.972)
  other arithmetic: 1.19 us -> 0.51 us
  Pallas kernels: 41.3 us -> 40.7 us
    mul x1, other arithmetic: 1.19 us -> 0.51 us  [shards(): return out.reshape(docs) * (1.0 / (docs * Y))]
    pallas_call x1, Pallas kernels: 41.3 us -> 40.7 us  [shards(): pl.pallas_call(functools.partial(kernel, math.sqrt(width)), out_shape=plt...]
where the time goes in v4:
time: 41.9 us; the launch traced here: 41.2 us
  Pallas kernels  40.7 us (97%)
  other arithmetic  0.51 us (1%)
    pallas_call x1, Pallas kernels, shards(): pl.pallas_call(functools.partial(kernel, math.sqrt(width)), out_shape=plt...  40.7 us

profile of v4, /device:TPU:1, one launch (start us, length us, event | category | flops | bytes accessed | tf_op | source)
XLA Modules:
  0.0 41.2 jit_solution(1591506383172989179)
XLA Ops:
  0.0 40.7 %shard_map.28 = f32[1,64]{1,0:T(1,128)S(1)} custom-call(bf16[64,1024]{1,0:T(8,128)(2,1)} %x_hbm.1, s32[1,64]{1,0:T(1,128)} %bitcast.3), custom_call_target="tpu_custom_call" | custom-call | tf_op jit(solution)/shard_map/pallas_call | solution.py:302
  40.7 0.5 %multiply_bitcast_fusion = f32[64]{0:T(128)} fusion(f32[1,64]{1,0:T(1,128)S(1)} %shard_map.28), kind=kLoop, calls=%fused_computation | loop fusion | flops 64 | bytes 512 | tf_op jit(solution)/shard_map/mul | solution.py:332

commit v5 on v4

--- a/solution.py
+++ b/solution.py
@@ -206,27 +206,34 @@
     starts = (ROWS, 2 * ROWS, 0, 3 * ROWS)
     targets = (None, partner, to_left, to_right)
 
-    def forward(which, g):
+    UNITS = [(0, 1), (1, 3), (3, 5), (5, 7), (7, 8)]
+
+    def forward(which, unit):
+        low, high = UNITS[unit]
+        at = pl.ds(low * RING, (high - low) * RING)
         return pltpu.make_async_remote_copy(
-            src_ref=middle.at[0] if g == 0 else raw.at[0, pl.ds(8 * g, 8)],
-            dst_ref=raw.at[which, pl.ds(8 * g, 8)],
-            send_sem=fwd_send.at[which - 1, g],
-            recv_sem=fwd_recv.at[which - 1, g],
+            src_ref=middle.at[0] if unit == 0 else raw.at[0, at],
+            dst_ref=raw.at[which, at],
+            send_sem=fwd_send.at[which - 1, unit],
+            recv_sem=fwd_recv.at[which - 1, unit],
             device_id=targets[which],
             device_id_type=MESH,
         )
 
-    for g in range(GROUPS):
-        if g > 0:
-            for piece in range(len(PIECES)):
-                along_second(g, piece).wait_recv()
+    for unit, (low, high) in enumerate(UNITS):
+        for b in range(low, high):
+            if b > 0:
+                for piece in range(len(PIECES)):
+                    along_second(b, piece).wait_recv()
         for which in (3, 2, 1):
-            forward(which, g).start()
-        convert(0, starts[0], g)
-    for g in range(GROUPS):
+            forward(which, unit).start()
+        for b in range(low, high):
+            convert(0, starts[0], b)
+    for unit, (low, high) in enumerate(UNITS):
         for which in (1, 2, 3):
-            forward(which, g).wait_recv()
-            convert(which, starts[which], g)
+            forward(which, unit).wait_recv()
+            for b in range(low, high):
+                convert(which, starts[which], b)
 
     from_r, own, mate, from_l = (pl.ds(start, ROWS) for start in (0, ROWS, 2 * ROWS, 3 * ROWS))
 
@@ -279,9 +286,9 @@
     for sent, sem in ((send_buf, one_send), (middle, two_send)):
         most = sent.at[pl.ds(1, RING - 1)]
         pltpu.make_async_copy(most, most, sem).wait()
-    for g in range(GROUPS):
+    for unit in range(len(UNITS)):
         for which in (1, 2, 3):
-            forward(which, g).wait_send()
+            forward(which, unit).wait_send()
     for which in range(3):
         part(which).wait_send()
     back = ret.at[pl.ds(1, SLOTS - 1)]

time: 41.9 us -> 41.5 us (level)
  no operation moved by 1% of the time
where the time goes in v5:
time: 41.5 us; the launch traced here: 41 us
  Pallas kernels  40.5 us (98%)
  other arithmetic  0.51 us (1%)
    pallas_call x1, Pallas kernels, shards(): pl.pallas_call(functools.partial(kernel, math.sqrt(width)), out_shape=plt...  40.5 us

profile of v5, /device:TPU:1, one launch (start us, length us, event | category | flops | bytes accessed | tf_op | source)
XLA Modules:
  0.0 41.0 jit_solution(6731200454356684528)
XLA Ops:
  0.0 40.5 %shard_map.28 = f32[1,64]{1,0:T(1,128)S(1)} custom-call(bf16[64,1024]{1,0:T(8,128)(2,1)} %x_hbm.1, s32[1,64]{1,0:T(1,128)} %bitcast.3), custom_call_target="tpu_custom_call" | custom-call | tf_op jit(solution)/shard_map/pallas_call | solution.py:309
  40.5 0.5 %multiply_bitcast_fusion = f32[64]{0:T(128)} fusion(f32[1,64]{1,0:T(1,128)S(1)} %shard_map.28), kind=kLoop, calls=%fused_computation | loop fusion | flops 64 | bytes 512 | tf_op jit(solution)/shard_map/mul | solution.py:339

commit v6 on v5

--- a/solution.py
+++ b/solution.py
@@ -225,7 +225,7 @@
             if b > 0:
                 for piece in range(len(PIECES)):
                     along_second(b, piece).wait_recv()
-        for which in (3, 2, 1):
+        for which in (2, 3, 1):
             forward(which, unit).start()
         for b in range(low, high):
             convert(0, starts[0], b)

time: 41.5 us -> 41.5 us (level)
  no operation moved by 1% of the time
where the time goes in v6:
time: 41.5 us; the launch traced here: 41 us
  Pallas kernels  40.5 us (98%)
  other arithmetic  0.51 us (1%)
    pallas_call x1, Pallas kernels, shards(): pl.pallas_call(functools.partial(kernel, math.sqrt(width)), out_shape=plt...  40.5 us

profile of v6, /device:TPU:1, one launch (start us, length us, event | category | flops | bytes accessed | tf_op | source)
XLA Modules:
  0.0 41.0 jit_solution(11523183628337000439)
XLA Ops:
  0.0 40.5 %shard_map.28 = f32[1,64]{1,0:T(1,128)S(1)} custom-call(bf16[64,1024]{1,0:T(8,128)(2,1)} %x_hbm.1, s32[1,64]{1,0:T(1,128)} %bitcast.3), custom_call_target="tpu_custom_call" | custom-call | tf_op jit(solution)/shard_map/pallas_call | solution.py:309
  40.5 0.5 %multiply_bitcast_fusion = f32[64]{0:T(128)} fusion(f32[1,64]{1,0:T(1,128)S(1)} %shard_map.28), kind=kLoop, calls=%fused_computation | loop fusion | flops 64 | bytes 512 | tf_op jit(solution)/shard_map/mul | solution.py:339
